TPU v7x, 768 devices: a whole 4x8x12 slice. The times are simulated.
768 devices in a mesh: edp: 48 (over z, x_lo, core), ep: 16 (over y, x_hi).
Axes of the slice: x: 4 (x_hi: 2, x_lo: 2; x = x_hi * 2 + x_lo), y: 8, z: 12, core: 2. Of those that a mesh axis runs over, the one named last changes fastest.
Arguments:
- route_ids: int32 [98304, 8], P(('edp', 'ep')), may hold values from 0 to 127, all different within a row; in each aligned block of 128 rows (0 to 127, 128 to 255, ...) at most 16 rows name the same one
- route_weights: float32 [98304, 8], P(('edp', 'ep')), may hold values from 0.02 to 0.5
- hidden: bfloat16 [48, 16, 16, 16, 384], P('edp', 'ep'), may hold values from -6 to 6
- down_weight: bfloat16 [16, 384, 2048], P('ep', 'edp'), may hold values from -0.3125 to 0.3125
- cotangent: bfloat16 [98304, 2048], P(('edp', 'ep')), may hold values from -6 to 6
Outputs:
- layer_out: bfloat16 [98304, 2048], P(('edp', 'ep'))
- route_grad: float32 [98304, 8], P(('edp', 'ep'))
- hidden_grad: bfloat16 [48, 16, 16, 16, 384], P('edp', 'ep')
- weight_grad: float32 [16, 384, 2048], P('ep', 'edp')
Inputs may be any that keep to these rules, and one draw needn't show every extreme that they name: `route_ids`: each row names 8 different experts; in the 128 rows of one device no expert is named by more than 16 rows.
All inputs are finite; a program needn't handle non-finite values.
Results may differ from a plain program's by a relative error of at most 0.0049.
Values may be sent and summed in bfloat16 or wider, within the bound.
A program may use at most 32 MiB of HBM per device.

v0:
```python
import jax
import jax.numpy as jnp
from jax import lax
from jax.sharding import Mesh
from jax.sharding import PartitionSpec as P

EDP = ("edp_0", "edp_1", "edp_2")
EDP_EP = ("edp_0", "edp_1", "edp_2", "ep")


def in_order(parts, dim):
    parts = jnp.moveaxis(parts, 0, dim)
    shape = parts.shape
    return parts.reshape(*shape[:dim], shape[dim] * shape[dim + 1], *shape[dim + 2 :])


def sent_to_all(value, axis):
    devices = lax.axis_size(axis)
    return lax.all_to_all(
        jnp.broadcast_to(value[None], (devices, *value.shape)), axis, 0, 0, tiled=True
    )


def gathered_copies(value, axis, dim):
    return in_order(sent_to_all(value, axis), dim)


def reduced_to_own(parts, axes, turns):
    inside = parts.shape[1:]
    parts = parts.reshape(*(lax.axis_size(a) for a in axes), *inside)
    parts = jnp.moveaxis(parts, turns, range(len(axes))).reshape(-1, *inside)
    for k in turns:
        parts = lax.psum_scatter(parts, axes[k], scatter_dimension=0, tiled=True)
    return parts[0]


def in_blocks(value, dim, devices):
    before, after = (value.shape[:dim], value.shape[dim + 1 :])
    return jnp.moveaxis(value.reshape(*before, devices, -1, *after), dim, 0)


def sum_by_axis(value, axes, turns, dim):
    devices = lax.axis_size(axes)
    return reduced_to_own(in_blocks(value, dim, devices), axes, turns)


def local(route_ids, route_weights, hidden, down_weight, cotangent):
    experts_here = lax.axis_size("ep")
    capacity = hidden.shape[3]
    features = cotangent.shape[1]
    hidden_width = hidden.shape[4]
    slot_total = hidden.shape[2] * capacity
    hidden_rows = hidden.reshape(slot_total, hidden_width)
    shard_rows = down_weight[0]
    weight_full = gathered_copies(shard_rows, EDP, 0)
    expert_out = jnp.dot(hidden_rows, weight_full, preferred_element_type=jnp.float32)
    sent_out = expert_out.astype(jnp.bfloat16).reshape(hidden.shape[2], capacity, features)
    arrived = lax.all_to_all(sent_out, "ep", split_axis=0, concat_axis=0, tiled=True)
    arrived_rows = arrived.reshape(experts_here * capacity, features)
    labels = jnp.arange(experts_here, dtype=jnp.int32)
    onehot = jnp.sum((route_ids[:, :, None] == labels).astype(jnp.int32), axis=1)
    preceding = jnp.cumsum(onehot, axis=0) - onehot
    flight = route_ids < experts_here
    expert = jnp.where(flight, route_ids, 0)
    slot_rank = jnp.take_along_axis(preceding, expert, axis=1)
    slot_index = expert * capacity + slot_rank
    mixing = jnp.where(flight, route_weights, jnp.float32(0.0))
    positions = jnp.arange(experts_here * capacity, dtype=jnp.int32)
    matches = (slot_index[None, :, :] == positions[:, None, None]) & flight[None, :, :]
    combine_table = jnp.sum(jnp.where(matches, mixing[None, :, :], jnp.float32(0.0)), axis=2)
    arrived_f32 = arrived_rows.astype(jnp.float32)
    combined = lax.dot_general(
        combine_table,
        arrived_f32,
        (((0,), (0,)), ((), ())),
        precision=lax.Precision.HIGHEST,
        preferred_element_type=jnp.float32,
    )
    scores = lax.dot_general(
        cotangent, arrived_rows, (((1,), (1,)), ((), ())), preferred_element_type=jnp.float32
    )
    route_grad = jnp.where(
        flight, jnp.take_along_axis(scores, slot_index, axis=1), jnp.float32(0.0)
    )
    selector = jnp.any(matches, axis=2).astype(jnp.bfloat16)
    slot_weight = jnp.sum(combine_table, axis=1)
    gathered_cot = jnp.dot(selector, cotangent, preferred_element_type=jnp.float32)
    slot_grad = (
        (gathered_cot * slot_weight[:, None])
        .astype(jnp.bfloat16)
        .reshape(experts_here, capacity, features)
    )
    returned = lax.all_to_all(slot_grad, "ep", split_axis=0, concat_axis=0, tiled=True)
    grad_rows = returned.reshape(slot_total, features)
    hidden_grad = lax.dot_general(
        grad_rows, weight_full, (((1,), (1,)), ((), ())), preferred_element_type=jnp.float32
    )
    hidden_grad = hidden_grad.astype(jnp.bfloat16).reshape(hidden.shape)
    local_grad = lax.dot_general(
        hidden_rows, grad_rows, (((0,), (0,)), ((), ())), preferred_element_type=jnp.float32
    )
    weight_grad = sum_by_axis(local_grad, EDP, (2, 0, 1), 0)
    return (combined.astype(jnp.bfloat16), route_grad, hidden_grad, weight_grad[None])


def solution(mesh):
    split = Mesh(
        mesh.devices.reshape(12, 2, 2, mesh.shape["ep"]), ("edp_0", "edp_1", "edp_2", "ep")
    )
    placed = (
        P(EDP_EP, None),
        P(EDP_EP, None),
        P(EDP, "ep", None, None, None),
        P("ep", EDP, None),
        P(EDP_EP, None),
    )
    return jax.shard_map(
        local,
        mesh=split,
        in_specs=placed,
        out_specs=(
            P(EDP_EP, None),
            P(EDP_EP, None),
            P(EDP, "ep", None, None, None),
            P("ep", EDP, None),
        ),
        check_vma=False,
    )
```

profile of v0, /device:TPU:1, one launch (start us, length us, event | category | flops | bytes accessed | tf_op | source)
XLA Modules:
  0.0 277.9 jit_solution(17198301848178006698)
XLA Ops:
  7.2 0.0 copy-start
  7.2 1.0 broadcast_in_dim.49
  8.2 0.0 copy-start.2
  8.2 76.8 %all_to_all.15 = bf16[48,8,2048]{2,1,0:T(8,128)(2,1)S(1)} all-to-all(bf16[48,8,2048]{2,1,0:T(8,128)(2,1)S(1)} %broadcast_in_dim.49), channel_id=1, replica_groups=mesh['edp_0'=12,'edp_1'=2,'edp_2'=2,'ep'=16] {'edp_0','edp_1','edp_2'}, dimensions={0} | all-to-all | bytes 3145728 | tf_op jit(solution)/shard_map/all_to_all | solution.py:19
  85.0 0.0 copy-done.2
  85.0 1.7 convolution_convert_fusion
  86.7 0.0 copy-start.4
  86.7 0.0 copy-start.5
  86.7 9.2 %all-to-all-start.1 = ((bf16[16,16,2048]{2,1,0:T(8,128)(2,1)}), bf16[16,16,2048]{2,1,0:T(8,128)(2,1)S(1)}, u32[]{:S(2)}, u32[]{:S(2)}) async-start(bf16[16,16,2048]{2,1,0:T(8,128)(2,1)} %bitcast.47), calls=%async_computation.1 | async-start | bytes 2097152 | tf_op jit(solution)/shard_map/all_to_all | solution.py:58
  95.9 0.0 reduce-scatter.4.cloned.1.call-start
  96.0 0.0 copy-done.4
  96.0 0.1 copy.20
  96.1 0.1 copy.22
  96.2 0.8 reduce_window_sum.11
  97.0 0.8 sub.3
  97.8 0.0 copy-done.5
  97.8 0.7 copy.26
  98.5 0.6 bitcast_or_fusion.1
  99.2 0.1 reshape.65
  99.3 0.8 copy.25
  100.0 7.1 %gather_fusion = s32[1024]{0:T(1024)S(1)} fusion(s32[128,16]{1,0:T(8,128)S(1)} %sub.3, s32[1024]{0:T(1024)S(1)} %reshape.65), kind=kCustom, calls=%fused_computation | custom fusion | bytes 16384 | tf_op jit(solution)/shard_map/jit(take_along_axis)/gather | solution.py:65
  107.1 0.1 reshape.68
  107.2 1.4 bitcast_or_fusion
  108.6 0.9 reshape.71
  109.6 1.0 fusion.8
  110.6 15.1 %all-to-all-done.1 = bf16[16,16,2048]{2,1,0:T(8,128)(2,1)S(1)} async-done(((bf16[16,16,2048]{2,1,0:T(8,128)(2,1)}), bf16[16,16,2048]{2,1,0:T(8,128)(2,1)S(1)}, u32[]{:S(2)}, u32[]{:S(2)}) %all-to-all-start.1) | async-done | bytes 1048608 | tf_op jit(solution)/shard_map/all_to_all | solution.py:58
  125.7 0.0 copy-done
  125.8 0.4 convolution_bitcast_fusion
  126.2 7.0 %gather_fusion.1 = f32[1024]{0:T(1024)S(1)} fusion(f32[128,256]{0,1:T(8,128)S(1)} %convolution_bitcast_fusion, s32[1024]{0:T(1024)S(1)} %reshape.71), kind=kCustom, calls=%fused_computation.1 | custom fusion | bytes 16384 | tf_op jit(solution)/shard_map/jit(take_along_axis)/gather | solution.py:83
  133.2 0.1 reshape.74
  133.3 1.5 select_select_fusion
  134.9 1.1 select_reduce_fusion
  135.9 1.2 fusion
  137.1 31.3 %all_to_all.16 = bf16[16,16,2048]{2,1,0:T(8,128)(2,1)S(1)} all-to-all(bf16[16,16,2048]{2,1,0:T(8,128)(2,1)S(1)} %bitcast.44), channel_id=1, replica_groups=mesh['edp_0'=12,'edp_1'=2,'edp_2'=2,'ep'=16] {'ep'}, dimensions={0} | all-to-all | bytes 2097152 | tf_op jit(solution)/shard_map/all_to_all | solution.py:93
  168.4 0.0 copy-start.1
  168.4 0.6 fusion.9
  169.1 0.4 copy-done.1
  169.5 1.9 copy.28
  171.3 0.0 reduce-scatter.4.cloned.1.call-update
  171.3 0.0 copy-start.3
  171.4 0.0 reduce-scatter.6.cloned.1.call-start
  171.4 13.7 %reduce-scatter.4.cloned.1.call-done = f32[24,8,2048]{2,1,0:T(8,128)} async-done(((f32[48,8,2048]{2,1,0:T(8,128)}), f32[24,8,2048]{2,1,0:T(8,128)}) %reduce-scatter.4.cloned.1.call-update) | async-done | bytes 1572880 | tf_op jit(solution)/shard_map/reduce_scatter | solution.py:33
  185.1 0.0 reduce-scatter.6.cloned.1.call-update
  185.2 0.0 reduce-scatter.8.cloned.1.call-start
  185.2 0.0 copy-done.3
  185.2 0.7 copy.29
  185.9 1.4 convolution_convert_fusion.1
  187.3 54.3 %reduce-scatter.6.cloned.1.call-done = f32[2,8,2048]{2,1,0:T(8,128)} async-done(((f32[24,8,2048]{2,1,0:T(8,128)}), f32[2,8,2048]{2,1,0:T(8,128)}) %reduce-scatter.6.cloned.1.call-update) | async-done | bytes 131088 | tf_op jit(solution)/shard_map/reduce_scatter | solution.py:33
  241.6 0.0 reduce-scatter.8.cloned.1.call-update
  241.6 2.6 fusion.4
  244.2 27.1 %reduce-scatter.8.cloned.1.call-done = f32[1,8,2048]{2,1,0:T(8,128)} async-done(((f32[2,8,2048]{2,1,0:T(8,128)}), f32[1,8,2048]{2,1,0:T(8,128)}) %reduce-scatter.8.cloned.1.call-update) | async-done | bytes 65552 | tf_op jit(solution)/shard_map/reduce_scatter | solution.py:33
  (3 shorter events, 0.1 us)
Async XLA Ops:
  7.2 118.6 %copy-start = (bf16[128,2048]{1,0:T(8,128)(2,1)S(1)}, bf16[128,2048]{1,0:T(8,128)(2,1)}, u32[]{:S(2)}) copy-start(bf16[128,2048]{1,0:T(8,128)(2,1)} %param.9) | copy-start | bytes 1572868
  8.2 76.8 %copy-start.2 = (bf16[1,1,16,16,384]{4,3,2,1,0:T(8,128)(2,1)S(1)}, bf16[1,1,16,16,384]{4,3,2,1,0:T(8,128)(2,1)}, u32[]{:S(2)}) copy-start(bf16[1,1,16,16,384]{4,3,2,1,0:T(8,128)(2,1)} %param.7) | copy-start | bytes 589828
  86.7 9.3 %copy-start.4 = (s32[128,8]{0,1:T(8,128)S(1)}, s32[128,8]{0,1:T(8,128)}, u32[]{:S(2)}) copy-start(s32[128,8]{0,1:T(8,128)} %param.5) | copy-start | bytes 12292
  86.7 11.1 %copy-start.5 = (f32[128,8]{0,1:T(8,128)S(1)}, f32[128,8]{0,1:T(8,128)}, u32[]{:S(2)}) copy-start(f32[128,8]{0,1:T(8,128)} %param.6) | copy-start | bytes 12292
  86.7 39.1 %all-to-all-start.1 = ((bf16[16,16,2048]{2,1,0:T(8,128)(2,1)}), bf16[16,16,2048]{2,1,0:T(8,128)(2,1)S(1)}, u32[]{:S(2)}, u32[]{:S(2)}) async-start(bf16[16,16,2048]{2,1,0:T(8,128)(2,1)} %bitcast.47), calls=%async_computation.1 | async-start | bytes 2097152 | tf_op jit(solution)/shard_map/all_to_all | solution.py:58
  95.9 89.2 %reduce-scatter.4.cloned.1.call-start = ((), (), s32[]{:S(2)}) async-start(), calls=%async_computation.6 | async-start | bytes 4718592 | tf_op jit(solution)/shard_map/reduce_scatter | solution.py:33
  168.4 1.0 copy-start.1
  171.3 13.9 %copy-start.3 = (f32[128,8]{1,0:T(8,128)S(1)}, f32[128,8]{1,0:T(8,128)}, u32[]{:S(2)}) copy-start(f32[128,8]{1,0:T(8,128)} %get-tuple-element.18) | copy-start | bytes 12292
  171.4 70.2 %reduce-scatter.6.cloned.1.call-start = ((), (), s32[]{:S(2)}) async-start(), calls=%async_computation.7 | async-start | bytes 1703936 | tf_op jit(solution)/shard_map/reduce_scatter | solution.py:33
  185.2 86.2 %reduce-scatter.8.cloned.1.call-start = ((), (), s32[]{:S(2)}) async-start(), calls=%async_computation.8 | async-start | bytes 196608 | tf_op jit(solution)/shard_map/reduce_scatter | solution.py:33
Sparse Core Ops, SparseCore 0:
  171.5 13.6 reduce-scatter.3
  188.3 53.2 reduce-scatter.5
  245.2 26.0 reduce-scatter.7
where the time goes:
time: 279 us; the launch traced here: 278 us
  waiting for transfers between devices  110 us (39%)
  blocking collectives  108 us (39%)
  local copies, waits for them, and re-layouts  21 us (8%)
  between operations  13.9 us (5%)
  starting transfers between devices  9.34 us (3%)
  matrix products  8 us (3%)
  other arithmetic  7.27 us (3%)
    reduce_scatter x3, waiting for transfers between devices, reduced_to_own(): parts = lax.psum_scatter(parts, axes[k], scatter_dimension=0, tiled=True)  95.1 us
    all_to_all x1, blocking collectives, sent_to_all(): lax.all_to_all(jnp.broadcast_to(value[None], (devices, *value.shape)), ax...  76.8 us
    all_to_all x1, blocking collectives, local(): lax.all_to_all(slot_grad, 'ep', split_axis=0, concat_axis=0, tiled=True)  31.3 us
    all_to_all x1, waiting for transfers between devices, local(): lax.all_to_all(sent_out, 'ep', split_axis=0, concat_axis=0, tiled=True)  15.1 us
    all_to_all x1, starting transfers between devices, local(): lax.all_to_all(sent_out, 'ep', split_axis=0, concat_axis=0, tiled=True)  9.22 us
    gather x3, local copies, waits for them, and re-layouts, local(): jnp.take_along_axis(scores, slot_index, axis=1)  8.03 us
    gather x3, local copies, waits for them, and re-layouts, local(): slot_rank = jnp.take_along_axis(preceding, expert, axis=1)  7.25 us
  transfers between devices with their start and end apart: 4, of which 4 were waited for; matrix products, arithmetic and copies ran while one was open for 7% of the time, Pallas kernels for 0%

commit v1 on v0

v1 whole, which is shorter than its diff:
```python
import functools

import jax
import jax.numpy as jnp
from jax import lax
from jax.experimental import pallas as pl
from jax.experimental.pallas import tpu as pltpu
from jax.sharding import Mesh
from jax.sharding import PartitionSpec as P

AXES = ("z", "xl", "c", "y", "xh")
EDP = ("z", "xl", "c")
EP = ("y", "xh")
MESH = pl.DeviceIdType.MESH
F32 = jnp.float32
BF16 = jnp.bfloat16


def centred(i, n):
    half = n // 2
    return lax.rem(half + (2 * lax.rem(i, 2) - 1) * ((i + 1) // 2), n)


def kernel(
    sizes,
    ids_ref, w_ref, hid_ref, wsh_ref, cot_ref,
    lo_ref, rg_ref, hg_ref, wg_ref,
    sg, gin, eo, arr, hidb, wsw, wf, hgp, hgr, hgo, pf, xs, xr, zs, zr, fs, fr, matched, mixing,
    hid_s, hid_r, hid_l, wsw_s, wsw_r, wz_s, wz_r, wx_s, wx_r,
    g_s, g_r, g_l, o_s, o_r, o_l, hg_s, hg_r, rx_s, rx_r, rz_s, rz_r, f_s, f_r,
):
    nz, ny, nxh = sizes
    ne = ny * nxh
    cap, half = sg.shape[2], sg.shape[3]
    slots = ne * cap
    tokens, top = ids_ref.shape
    z, xl, c = lax.axis_index("z"), lax.axis_index("xl"), lax.axis_index("c")
    y, xh = lax.axis_index("y"), lax.axis_index("xh")
    me = y * nxh + xh
    core = 1 - c
    chip = z * 2 + xl

    def remote(src, dst, send, recv, **where):
        return pltpu.make_async_remote_copy(
            src_ref=src, dst_ref=dst, send_sem=send, recv_sem=recv,
            device_id=where, device_id_type=MESH,
        )

    barrier = pltpu.get_barrier_semaphore()

    def tell(**where):
        pl.semaphore_signal(barrier, inc=1, device_id=where, device_id_type=MESH)

    def tell_z(i, carry):
        tell(z=lax.rem(z + centred(i, nz), nz))
        return carry

    def tell_y(i, carry):
        yy = lax.rem(y + centred(i, ny), ny)
        for x in range(nxh):
            for h in range(2):
                tell(y=yy, xh=x, c=h)
        return carry

    lax.fori_loop(0, ny - 1, tell_y, 0)
    lax.fori_loop(0, nz - 1, tell_z, 0)
    tell(xl=1 - xl)
    for dx in range(1, nxh):
        for h in range(2):
            tell(xh=lax.rem(xh + dx, nxh), c=h)
    tell(c=core)
    peers = (ny - 1) * nxh * 2 + (nz - 1) + 1 + (nxh - 1) * 2 + 1

    ids = ids_ref[...]
    weights = w_ref[...]
    position = lax.broadcasted_iota(jnp.int32, (tokens, slots), 1)
    expert_of = position // cap
    rank_of = position - expert_of * cap
    names = jnp.zeros((tokens, slots), F32)
    chosen = jnp.zeros((tokens, slots), F32)
    for k in range(top):
        hit = ids[:, k : k + 1] == expert_of
        names = jnp.where(hit, 1.0, names)
        chosen = jnp.where(hit, weights[:, k : k + 1], chosen)
    row = lax.broadcasted_iota(jnp.int32, (tokens, tokens), 0)
    col = lax.broadcasted_iota(jnp.int32, (tokens, tokens), 1)
    before = jnp.where(col < row, 1.0, 0.0).astype(BF16)
    preceding = jnp.dot(before, names.astype(BF16), preferred_element_type=F32)
    match = jnp.where((names > 0.5) & (preceding == rank_of.astype(F32)), 1.0, 0.0)
    mix = match * chosen
    matched[...] = match
    mixing[...] = mix
    selector = match.T.astype(BF16)
    slot_weight = jnp.sum(mix.T, axis=1, keepdims=True)
    piece = min(half, 512)
    for h in range(2):
        for p in range(half // piece):
            at = h * half + p * piece
            picked = jnp.dot(selector, cot_ref[:, at : at + piece], preferred_element_type=F32)
            sg[h, :, :, p * piece : (p + 1) * piece] = (
                (picked * slot_weight).astype(BF16).reshape(ne, cap, piece)
            )

    pl.semaphore_wait(barrier, peers)

    other_half = pl.ds(pl.multiple_of(core * half, half), half)
    own_half = pl.ds(pl.multiple_of(c * half, half), half)
    swap = remote(wsh_ref.at[:, other_half], wsw, wsw_s, wsw_r, c=core)
    swap.start()
    share = remote(hid_ref, hidb.at[c], hid_s, hid_r, c=core)
    share.start()
    keep = pltpu.make_async_copy(hid_ref, hidb.at[c], hid_l)
    keep.start()

    def exchange(src, dst, send, recv, by_dest_core):
        slot = c * ne + me

        def to(yy, x, h):
            remote(src.at[h, yy * nxh + x], dst.at[slot], send, recv, y=yy, xh=x, c=h).start()

        def ring(i, carry):
            yy = lax.rem(y + centred(i, ny), ny)
            for x in range(nxh):
                for h in range(2):
                    to(yy, x, h)
            return carry

        lax.fori_loop(0, ny - 1, ring, 0)
        for dx in range(1, nxh):
            for h in range(2):
                to(y, lax.rem(xh + dx, nxh), h)
        to(y, xh, core)

    rest = 2 * ne - 1

    def all_of(ref, sem, count):
        pltpu.make_async_copy(ref.at[pl.ds(0, count)], ref.at[pl.ds(0, count)], sem).wait()

    swap.wait_recv()
    mine = wsh_ref[:, own_half].astype(F32)
    theirs = wsw[...].astype(F32)
    first = jnp.where(c == 0, mine, theirs)
    second = jnp.where(c == 0, theirs, mine)
    wf[chip] = jnp.concatenate([first, second], axis=0).astype(BF16)

    def spread(i, carry):
        d = centred(i, nz)
        remote(wf.at[chip], wf.at[chip], wz_s, wz_r.at[i], z=lax.rem(z + d, nz)).start()
        return carry

    lax.fori_loop(0, nz - 1, spread, 0)
    remote(wf.at[chip], wf.at[chip], wx_s, wx_r, xl=1 - xl).start()
    exchange(sg, gin, g_s, g_r, True)
    stay = pltpu.make_async_copy(sg.at[c, me], gin.at[c * ne + me], g_l)
    stay.start()

    def forward(i, carry):
        d = centred(i, nz)
        at = lax.rem(z - d + nz, nz) * 2 + xl
        remote(wf.at[at], wf.at[at], wz_s, wz_r.at[i], z=lax.rem(z + d, nz)).wait_recv()
        remote(wf.at[at], wf.at[at], wx_s, wx_r, xl=1 - xl).start()
        return carry

    lax.fori_loop(0, nz - 1, forward, 0)
    all_of(wf, wx_r, nz)
    share.wait_recv()
    keep.wait()

    ff = wf.shape[0] * wf.shape[1]

    def outputs(i, carry):
        n = pl.ds(pl.multiple_of(i * 256, 256), 256) if half >= 256 else slice(None)
        wide = min(half, 256)
        for h in range(2):
            got = jnp.dot(
                hidb[h], wf[:, :, n].reshape(ff, wide), preferred_element_type=F32
            )
            eo[h, :, :, n] = got.astype(BF16).reshape(ne, cap, wide)
        return carry

    lax.fori_loop(0, max(1, half // 256), outputs, 0)
    exchange(eo, arr, o_s, o_r, False)
    stay_out = pltpu.make_async_copy(eo.at[c, me], arr.at[c * ne + me], o_l)
    stay_out.start()

    all_of(gin, g_r, rest)
    stay.wait()

    def products(i, carry):
        n = pl.ds(pl.multiple_of(i * 256, 256), 256) if half >= 256 else slice(None)
        wide = min(half, 256)
        got = lax.dot_general(
            hidb[...].reshape(2 * slots, ff),
            gin[:, :, n].reshape(2 * slots, wide),
            (((0,), (0,)), ((), ())),
            preferred_element_type=F32,
        )
        pf[:, :, :, n] = got.reshape(*pf.shape[:3], wide)
        return carry

    lax.fori_loop(0, max(1, half // 256), products, 0)

    def to_neighbour(i, carry):
        to = lax.rem(z + centred(i, nz), nz)
        xs[to] = pf[to, 1 - xl].astype(BF16)
        remote(xs.at[to], xr.at[to], rx_s, rx_r.at[i], xl=1 - xl).start()
        return carry

    lax.fori_loop(0, nz, to_neighbour, 0)

    def hidden_term(group):
        rows = gin[pl.ds(group * ne, ne)].reshape(slots, half)
        return lax.dot_general(
            rows, wf[...].reshape(ff, half), (((1,), (1,)), ((), ())), preferred_element_type=F32
        )

    hgp[...] = hidden_term(core)
    give = remote(hgp, hgr, hg_s, hg_r, c=core)
    give.start()
    hgo[...] = hidden_term(c)

    def along_z(i, carry):
        to = lax.rem(z + centred(i, nz), nz)
        remote(xs.at[to], xr.at[to], rx_s, rx_r.at[i], xl=1 - xl).wait_recv()
        zs[to] = (pf[to, xl] + xr[to].astype(F32)).astype(BF16)
        remote(zs.at[to], zr.at[z], rz_s, rz_r, z=to).start()
        return carry

    lax.fori_loop(0, nz - 1, along_z, 0)
    remote(xs.at[z], xr.at[z], rx_s, rx_r.at[nz - 1], xl=1 - xl).wait_recv()
    total = pf[z, xl] + xr[z].astype(F32)

    give.wait_recv()
    hg_ref[...] = (hgo[...] + hgr[...]).astype(BF16)

    all_of(zr, rz_r, nz - 1)
    for d in range(1, nz):
        total = total + zr[lax.rem(z + d, nz)].astype(F32)
    rows = total.shape[0] // 2
    fs[...] = jnp.where(c == 0, total[rows:], total[:rows])
    finish = remote(fs, fr, f_s, f_r, c=core)
    finish.start()
    own_rows = jnp.where(c == 0, total[:rows], total[rows:])
    wg_ref[:, own_half] = own_rows
    finish.wait_recv()
    wg_ref[:, other_half] = fr[...]

    all_of(arr, o_r, rest)
    stay_out.wait()
    mix = mixing[...]
    high = mix.astype(BF16)
    low = (mix - high.astype(F32)).astype(BF16)
    table = jnp.concatenate([high, low], axis=0)
    for h in range(2):
        for p in range(half // piece):
            part = arr[h * ne : (h + 1) * ne, :, p * piece : (p + 1) * piece]
            both = jnp.dot(table, part.reshape(slots, piece), preferred_element_type=F32)
            at = h * half + p * piece
            lo_ref[:, at : at + piece] = (both[:tokens] + both[tokens:]).astype(BF16)
    scores = jnp.zeros((tokens, slots), F32)
    for h in range(2):
        scores = scores + lax.dot_general(
            cot_ref[:, h * half : (h + 1) * half],
            arr[h * ne : (h + 1) * ne].reshape(slots, half),
            (((1,), (1,)), ((), ())),
            preferred_element_type=F32,
        )
    scores = jnp.where(matched[...] > 0.5, scores, 0.0)
    lane = lax.broadcasted_iota(jnp.int32, (tokens, top), 1)
    grad = jnp.zeros((tokens, top), F32)
    for k in range(top):
        value = jnp.sum(
            jnp.where(ids[:, k : k + 1] == expert_of, scores, 0.0), axis=1, keepdims=True
        )
        grad = jnp.where(lane == k, value, grad)
    rg_ref[...] = grad

    swap.wait_send()
    share.wait_send()
    give.wait_send()
    finish.wait_send()
    all_of(wf, wz_s, nz - 1)
    all_of(wf, wx_s, nz)
    all_of(gin, g_s, rest)
    all_of(arr, o_s, rest)
    all_of(xs, rx_s, nz)
    all_of(zs, rz_s, nz - 1)


def solution(mesh):
    nz = mesh.shape["edp"] // 4
    ny = mesh.shape["ep"] // 2
    split = Mesh(mesh.devices.reshape(nz, 2, 2, ny, 2), AXES)

    def local(route_ids, route_weights, hidden, down_weight, cotangent):
        tokens, top = route_ids.shape
        ne, cap, ff = hidden.shape[2:]
        rows, features = down_weight.shape[1:]
        half = features // 2
        slots = ne * cap
        vmem = pl.BlockSpec(memory_space=pltpu.VMEM)
        dma = pltpu.SemaphoreType.DMA
        outs = pl.pallas_call(
            functools.partial(kernel, (nz, ny, 2)),
            out_shape=(
                jax.ShapeDtypeStruct((tokens, features), BF16),
                jax.ShapeDtypeStruct((tokens, top), F32),
                jax.ShapeDtypeStruct((slots, ff), BF16),
                jax.ShapeDtypeStruct((rows, features), F32),
            ),
            in_specs=[vmem] * 5,
            out_specs=(vmem,) * 4,
            scratch_shapes=[
                pltpu.VMEM((2, ne, cap, half), BF16),
                pltpu.VMEM((2 * ne, cap, half), BF16),
                pltpu.VMEM((2, ne, cap, half), BF16),
                pltpu.VMEM((2 * ne, cap, half), BF16),
                pltpu.VMEM((2, slots, ff), BF16),
                pltpu.VMEM((rows, half), BF16),
                pltpu.VMEM((2 * nz, 2 * rows, half), BF16),
                pltpu.VMEM((slots, ff), F32),
                pltpu.VMEM((slots, ff), F32),
                pltpu.VMEM((slots, ff), F32),
                pltpu.VMEM((nz, 2, 2 * rows, half), F32),
                pltpu.VMEM((nz, 2 * rows, half), BF16),
                pltpu.VMEM((nz, 2 * rows, half), BF16),
                pltpu.VMEM((nz, 2 * rows, half), BF16),
                pltpu.VMEM((nz, 2 * rows, half), BF16),
                pltpu.VMEM((rows, half), F32),
                pltpu.VMEM((rows, half), F32),
                pltpu.VMEM((tokens, slots), F32),
                pltpu.VMEM((tokens, slots), F32),
                dma, dma, dma,
                dma, dma,
                dma, dma((nz - 1,)), dma, dma,
                dma, dma, dma,
                dma, dma, dma,
                dma, dma,
                dma, dma((nz,)),
                dma, dma,
                dma, dma,
            ],
            compiler_params=pltpu.CompilerParams(
                collective_id=0, has_side_effects=True, vmem_limit_bytes=60 * 2**20
            ),
        )(
            route_ids,
            route_weights,
            hidden.reshape(slots, ff),
            down_weight.reshape(rows, features),
            cotangent,
        )
        out, route_grad, hidden_grad, weight_grad = outs
        return out, route_grad, hidden_grad.reshape(hidden.shape), weight_grad[None]

    placed = (P(AXES, None), P(AXES, None), P(EDP, EP, None, None, None), P(EP, EDP, None), P(AXES, None))
    return jax.shard_map(
        local,
        mesh=split,
        in_specs=placed,
        out_specs=(P(AXES, None), P(AXES, None), P(EDP, EP, None, None, None), P(EP, EDP, None)),
        check_vma=False,
    )
```

time: 279 us -> 85.1 us (0.31)
  waiting for transfers between devices: 110 us -> 0 us
  blocking collectives: 108 us -> 0 us
  Pallas kernels: 0 us -> 76.7 us
  local copies, waits for them, and re-layouts: 21 us -> 7.07 us
  between operations: 13.9 us -> 0.65 us
  starting transfers between devices: 9.34 us -> 0 us
  matrix products: 8 us -> 0 us
  other arithmetic: 7.27 us -> 0 us
    all_to_all x2 -> x0, blocking collectives: 108 us -> none  [the longest x1 76.8 us: sent_to_all(): lax.all_to_all(jnp.broadcast_to(value[None], (devices, *value.shape)), ax...]
    reduce_scatter x3 -> x0, waiting for transfers between devices: 95.1 us -> none  [reduced_to_own(): parts = lax.psum_scatter(parts, axes[k], scatter_dimension=0, tiled=True)]
    pallas_call x0 -> x1, Pallas kernels: none -> 76.7 us  [local(): pl.pallas_call(functools.partial(kernel, (nz, ny, 2)), out_shape=(jax.Sha...]
    gather x6 -> x0, local copies, waits for them, and re-layouts: 15.3 us -> none  [the longest x3 8.03 us: local(): jnp.take_along_axis(scores, slot_index, axis=1)]
    all_to_all x1 -> x0, waiting for transfers between devices: 15.1 us -> none  [local(): lax.all_to_all(sent_out, 'ep', split_axis=0, concat_axis=0, tiled=True)]
    all_to_all x1 -> x0, starting transfers between devices: 9.22 us -> none  [local(): lax.all_to_all(sent_out, 'ep', split_axis=0, concat_axis=0, tiled=True)]
    dot_general x6 -> x0, matrix products: 8 us -> none  [the longest x1 2.63 us: local(): lax.dot_general(grad_rows, weight_full, (((1,), (1,)), ((), ())), preferr...]
    unnamed x15 -> x12, local copies, waits for them, and re-layouts: 1.92 us -> 7.07 us
  transfers between devices with their start and end apart: 4 -> 0, of which waited for: 4 -> 0; matrix products, arithmetic and copies ran while one was open for 7% -> 0% of each run, Pallas kernels for 0% -> 0%
where the time goes in v1:
time: 85.1 us; the launch traced here: 84.4 us
  Pallas kernels  76.7 us (90%)
  local copies, waits for them, and re-layouts  7.07 us (8%)
    pallas_call x1, Pallas kernels, local(): pl.pallas_call(functools.partial(kernel, (nz, ny, 2)), out_shape=(jax.Sha...  76.7 us
    unnamed x12, local copies, waits for them, and re-layouts  7.07 us

profile of v1, /device:TPU:1, one launch (start us, length us, event | category | flops | bytes accessed | tf_op | source)
XLA Modules:
  0.0 84.4 jit_solution(4590786450318276987)
XLA Ops:
  0.6 0.0 copy-start.2
  0.6 1.4 %copy.9.ids_ref = s32[128,8]{1,0:T(8,128)} copy(s32[128,8]{0,1:T(8,128)} %param.5) | data formatting | bytes 8192 | tf_op args[0]
  2.1 0.0 copy-done.2
  2.1 0.7 copy.10.w_ref
  2.8 76.7 %shard_map.84 = (bf16[128,2048]{1,0:T(8,128)(2,1)}, f32[128,8]{1,0:T(8,128)}, bf16[256,384]{1,0:T(8,128)(2,1)}, f32[8,2048]{1,0:T(8,128)}) custom-call(s32[128,8]{1,0:T(8,128)} %copy.9.ids_ref, f32[128,8]{1,0:T(8,128)} %copy.10.w_ref, bf16[256,384]{1,0:T(8,128)(2,1)} %bitcast.4, bf16[8,2048]{1,0:T(8,128)(2,1)} %bitcast.7, bf16[128,2048]{1,0:T(8,128)(2,1)} %cot_ref.1), custom_call_target="tpu_custom_call" | custom-call | tf_op jit(solution)/shard_map/pallas_call | solution.py:303
  79.5 1.5 %copy.11 = f32[128,8]{0,1:T(8,128)} copy(f32[128,8]{1,0:T(8,128)} %get-tuple-element.13) | data formatting | bytes 8192
  81.0 0.0 copy-start
  81.0 1.9 %copy.15 = bf16[128,2048]{1,0:T(8,128)(2,1)} copy(bf16[128,2048]{1,0:T(8,128)(2,1)} %get-tuple-element.20) | data formatting | bytes 1048576
  82.9 0.0 copy-done
  82.9 0.0 copy-start.1
  82.9 0.7 copy.16
  83.6 0.2 copy-done.1
  83.8 0.6 copy.17
Async XLA Ops:
  0.6 1.4 %copy-start.2 = (f32[128,8]{0,1:T(8,128)S(1)}, f32[128,8]{0,1:T(8,128)}, u32[]{:S(2)}) copy-start(f32[128,8]{0,1:T(8,128)} %param.6) | copy-start | bytes 12292
  81.0 1.9 %copy-start = (bf16[256,384]{1,0:T(8,128)(2,1)S(1)}, bf16[256,384]{1,0:T(8,128)(2,1)}, u32[]{:S(2)}) copy-start(bf16[256,384]{1,0:T(8,128)(2,1)} %get-tuple-element.10) | copy-start | bytes 589828
  82.9 0.9 %copy-start.1 = (f32[8,2048]{1,0:T(8,128)S(1)}, f32[8,2048]{1,0:T(8,128)}, u32[]{:S(2)}) copy-start(f32[8,2048]{1,0:T(8,128)} %get-tuple-element.11) | copy-start | bytes 196612

commit v2 on v1

v2 whole, which is shorter than its diff:
```python
import functools

import jax
import jax.numpy as jnp
from jax import lax
from jax.experimental import pallas as pl
from jax.experimental.pallas import tpu as pltpu
from jax.sharding import Mesh
from jax.sharding import PartitionSpec as P

AXES = ("z", "xl", "c", "y", "xh")
EDP = ("z", "xl", "c")
EP = ("y", "xh")
MESH = pl.DeviceIdType.MESH
F32 = jnp.float32
BF16 = jnp.bfloat16


ORDER = (1, -1, 4, -4, 2, -2, 3, -3, 5, -5, 6)


def centred(i, n):
    half = n // 2
    return lax.rem(half + (2 * lax.rem(i, 2) - 1) * ((i + 1) // 2), n)


def kernel(
    sizes,
    ids_ref, w_ref, hid_ref, wsh_ref, cot_ref,
    lo_ref, rg_ref, hg_ref, wg_ref,
    cot, own_w, sg, gin, eo, arr, hidb, wsw, wf, hgp, hgr, hgo, pf, xs, xr, zs, zr, fs, fr,
    matched, mixing,
    clear,
    cot_l, ow_l, hid_s, hid_r, hid_l, wsw_s, wsw_r, wz_s, wz_r, wx_s, wx_r,
    g_s, g_r, g_l, o_s, o_r, o_l, hg_s, hg_r, rx_s, rx_r, rz_s, rz_r, f_s, f_r,
):
    nz, ny, nxh, early = sizes
    chunks, _, ne, cap, wide = sg.shape
    half = chunks * wide
    slots = ne * cap
    top, tokens = ids_ref.shape
    ff = wf.shape[0] * wf.shape[1]
    z, xl, c = lax.axis_index("z"), lax.axis_index("xl"), lax.axis_index("c")
    y, xh = lax.axis_index("y"), lax.axis_index("xh")
    me = y * nxh + xh
    core = 1 - c
    chip = z * 2 + xl
    own_slot = c * ne + me

    def remote(src, dst, send, recv, **where):
        return pltpu.make_async_remote_copy(
            src_ref=src, dst_ref=dst, send_sem=send, recv_sem=recv,
            device_id=where, device_id_type=MESH,
        )

    def tell(sem, **where):
        pl.semaphore_signal(sem, inc=1, device_id=where, device_id_type=MESH)

    def all_of(ref, sem, count):
        pltpu.make_async_copy(ref.at[pl.ds(0, count)], ref.at[pl.ds(0, count)], sem).wait()

    barrier = pltpu.get_barrier_semaphore()

    def tell_y(i, carry):
        yy = lax.rem(y + centred(i, ny), ny)
        for x in range(nxh):
            for h in range(2):
                tell(barrier, y=yy, xh=x, c=h)
        return carry

    lax.fori_loop(0, ny - 1, tell_y, 0)
    for dx in range(1, nxh):
        for h in range(2):
            tell(barrier, xh=lax.rem(xh + dx, nxh), c=h)
    tell(barrier, xl=1 - xl)
    tell(barrier, c=core)

    late = z >= early

    def tell_z(i, carry):
        zz = lax.rem(z + centred(i, nz), nz)

        @pl.when((zz >= early) | jnp.logical_not(late))
        def _():
            tell(barrier, z=zz)

        return carry

    lax.fori_loop(0, nz - 1, tell_z, 0)
    plane = (ny - 1) * nxh * 2 + (nxh - 1) * 2 + 2
    peers = plane + jnp.where(late, nz - 1, early - 1)

    load_cot = pltpu.make_async_copy(cot_ref, cot, cot_l)
    load_cot.start()
    load_w = pltpu.make_async_copy(wsh_ref, own_w, ow_l)
    load_w.start()
    keep = pltpu.make_async_copy(hid_ref, hidb.at[c], hid_l)
    keep.start()

    ids = ids_ref[...]
    weights = w_ref[...]
    position = lax.broadcasted_iota(jnp.int32, (slots, tokens), 0)
    expert_of = position // cap
    rank_of = position - expert_of * cap
    names = jnp.zeros((slots, tokens), F32)
    chosen = jnp.zeros((slots, tokens), F32)
    for k in range(top):
        hit = ids[k : k + 1, :] == expert_of
        names = jnp.where(hit, 1.0, names)
        chosen = jnp.where(hit, weights[k : k + 1, :], chosen)
    row = lax.broadcasted_iota(jnp.int32, (tokens, tokens), 0)
    col = lax.broadcasted_iota(jnp.int32, (tokens, tokens), 1)
    before = jnp.where(row < col, 1.0, 0.0).astype(BF16)
    preceding = jnp.dot(names.astype(BF16), before, preferred_element_type=F32)
    match = jnp.where((names > 0.5) & (preceding == rank_of.astype(F32)), 1.0, 0.0)
    mix = match * chosen
    matched[...] = match
    selector = match.astype(BF16)
    slot_weight = jnp.sum(mix, axis=1, keepdims=True)
    load_cot.wait()

    def weigh(q):
        for h in range(2):
            at = h * half + q * wide
            picked = jnp.dot(selector, cot[:, at : at + wide], preferred_element_type=F32)
            sg[q, h] = (picked * slot_weight).astype(BF16).reshape(ne, cap, wide)

    weigh(0)

    pl.semaphore_wait(barrier, peers)

    @pl.when(late)
    def _():
        for zz in range(early):
            tell(clear, z=zz)

    load_w.wait()
    other_half = pl.ds(pl.multiple_of(core * half, half), half)
    own_half = pl.ds(pl.multiple_of(c * half, half), half)
    swap = remote(own_w.at[:, other_half], wsw, wsw_s, wsw_r, c=core)
    swap.start()

    def near(src, dst, send, recv):
        def ring(i, carry):
            yy = lax.rem(y + centred(i, ny), ny)
            for h in range(2):
                remote(src.at[h, yy * nxh + xh], dst.at[own_slot], send, recv, y=yy, c=h).start()
            return carry

        lax.fori_loop(0, ny - 1, ring, 0)
        remote(src.at[core, me], dst.at[own_slot], send, recv, c=core).start()

    def far_step(i, src, dst, send, recv):
        yy = lax.rem(y + centred(i, ny), ny)
        for dx in range(1, nxh):
            xx = lax.rem(xh + dx, nxh)
            for h in range(2):
                remote(
                    src.at[h, yy * nxh + xx], dst.at[own_slot], send, recv, y=yy, xh=xx, c=h
                ).start()

    def far(src, dst, send, recv):
        def ring(i, carry):
            far_step(i, src, dst, send, recv)
            return carry

        lax.fori_loop(0, ny, ring, 0)

    rest = 2 * ne - 1
    stay = [pltpu.make_async_copy(sg.at[q, c, me], gin.at[q, own_slot], g_l.at[q]) for q in range(chunks)]
    near(sg.at[0], gin.at[0], g_s, g_r.at[0])
    stay[0].start()
    far(sg.at[0], gin.at[0], g_s, g_r.at[0])
    share = remote(hid_ref, hidb.at[c], hid_s, hid_r, c=core)
    share.start()
    for q in range(1, chunks):
        weigh(q)
        near(sg.at[q], gin.at[q], g_s, g_r.at[q])
        stay[q].start()
        far(sg.at[q], gin.at[q], g_s, g_r.at[q])

    swap.wait_recv()
    mine = own_w[:, own_half].astype(F32)
    theirs = wsw[...].astype(F32)
    first = jnp.where(c == 0, mine, theirs)
    second = jnp.where(c == 0, theirs, mine)
    wf[chip] = jnp.concatenate([first, second], axis=0).astype(BF16)
    remote(wf.at[chip], wf.at[chip], wx_s, wx_r, xl=1 - xl).start()
    mixing[...] = mix.T

    @pl.when(jnp.logical_not(late))
    def _():
        pl.semaphore_wait(clear, nz - early)

    def pass_on(piece, d, step):
        remote(
            wf.at[piece], wf.at[piece], wz_s, wz_r.at[ORDER.index(d)], z=lax.rem(z + step + nz, nz)
        ).start()

    for d in (4, -4, 1, -1):
        pass_on(chip, d, d)
    last = chunks - 1

    for i, d in enumerate(ORDER):
        at = lax.rem(z - d + nz, nz) * 2 + xl
        remote(wf.at[at], wf.at[at], wz_s, wz_r.at[i], xl=1 - xl).wait_recv()
        if abs(d) == 1:
            pass_on(at, 2 * d, d)
        if abs(d) == 4:
            sign = d // 4
            pass_on(at, 5 * sign, sign)
            pass_on(at, 3 * sign, -sign)

            @pl.when(c == (1 - sign) // 2)
            def _():
                pass_on(at, 6, 2 * sign)

        remote(wf.at[at], wf.at[at], wx_s, wx_r, xl=1 - xl).start()

    def products(q):
        step = min(wide, 256)

        def body(i, carry):
            n = pl.ds(pl.multiple_of(i * step, step), step)
            got = lax.dot_general(
                hidb[...].reshape(2 * slots, ff),
                gin[q, :, :, n].reshape(2 * slots, step),
                (((0,), (0,)), ((), ())),
                preferred_element_type=F32,
            )
            pf[q, :, :, :, n] = got.reshape(nz, 2, pf.shape[3], step)
            return carry

        lax.fori_loop(0, wide // step, body, 0)

        def to_neighbour(i, carry):
            to = lax.rem(z + centred(i, nz), nz)
            xs[q, to] = pf[q, to, 1 - xl].astype(BF16)
            remote(xs.at[q, to], xr.at[q, to], rx_s, rx_r.at[q, i], xl=1 - xl).start()
            return carry

        lax.fori_loop(0, nz, to_neighbour, 0)

    def along_z(q):
        def body(i, carry):
            to = lax.rem(z + centred(i, nz), nz)
            remote(xs.at[q, to], xr.at[q, to], rx_s, rx_r.at[q, i], xl=1 - xl).wait_recv()
            zs[q, to] = (pf[q, to, xl] + xr[q, to].astype(F32)).astype(BF16)
            remote(zs.at[q, to], zr.at[q, z], rz_s, rz_r.at[q], z=to).start()
            return carry

        lax.fori_loop(0, nz - 1, body, 0)

    def outputs():
        step = min(half, 256)

        def body(i, carry):
            n = pl.ds(pl.multiple_of(i * step, step), step)
            for h in range(2):
                got = jnp.dot(
                    hidb[h], wf[:, :, n].reshape(ff, step), preferred_element_type=F32
                )
                eo[h, :, :, n] = got.astype(BF16).reshape(ne, cap, step)
            return carry

        lax.fori_loop(0, half // step, body, 0)

    share.wait_recv()
    keep.wait()
    for q in range(chunks):
        all_of(gin.at[q], g_r.at[q], rest)
        stay[q].wait()
        if q == last:
            near(eo, arr, o_s, o_r)
        products(q)
        if q == 0:
            all_of(wf, wx_r, nz)
            outputs()
        if q < chunks - 1:
            along_z(q)
    stay_out = pltpu.make_async_copy(eo.at[c, me], arr.at[own_slot], o_l)
    stay_out.start()
    far(eo, arr, o_s, o_r)
    along_z(last)

    def hidden_term(group):
        got = jnp.zeros((slots, ff), F32)
        for q in range(chunks):
            rows = gin[q, pl.ds(group * ne, ne)].reshape(slots, wide)
            cols = wf[:, :, q * wide : (q + 1) * wide].reshape(ff, wide)
            got = got + lax.dot_general(
                rows, cols, (((1,), (1,)), ((), ())), preferred_element_type=F32
            )
        return got

    hgp[...] = hidden_term(core)
    give = remote(hgp, hgr, hg_s, hg_r, c=core)
    give.start()
    hgo[...] = hidden_term(c)
    give.wait_recv()
    hg_ref[...] = (hgo[...] + hgr[...]).astype(BF16)

    rows = fs.shape[0]
    for q in range(chunks):
        remote(
            xs.at[q, z], xr.at[q, z], rx_s, rx_r.at[q, nz - 1], xl=1 - xl
        ).wait_recv()
        total = pf[q, z, xl] + xr[q, z].astype(F32)
        all_of(zr.at[q], rz_r.at[q], nz - 1)
        for d in range(1, nz):
            total = total + zr[q, lax.rem(z + d, nz)].astype(F32)
        fs[:, q * wide : (q + 1) * wide] = jnp.where(c == 0, total[rows:], total[:rows])
        at = pl.multiple_of(c * half + q * wide, wide)
        wg_ref[:, pl.ds(at, wide)] = jnp.where(c == 0, total[:rows], total[rows:])
    finish = remote(fs, fr, f_s, f_r, c=core)
    finish.start()

    all_of(arr, o_r, rest)
    stay_out.wait()
    mix = mixing[...]
    high = mix.astype(BF16)
    low = (mix - high.astype(F32)).astype(BF16)
    table = jnp.concatenate([high, low], axis=0)
    piece = min(half, 512)
    for h in range(2):
        for p in range(half // piece):
            part = arr[h * ne : (h + 1) * ne, :, p * piece : (p + 1) * piece]
            both = jnp.dot(table, part.reshape(slots, piece), preferred_element_type=F32)
            at = h * half + p * piece
            lo_ref[:, at : at + piece] = (both[:tokens] + both[tokens:]).astype(BF16)
    scores = jnp.zeros((slots, tokens), F32)
    for h in range(2):
        scores = scores + lax.dot_general(
            arr[h * ne : (h + 1) * ne].reshape(slots, half),
            cot[:, h * half : (h + 1) * half],
            (((1,), (1,)), ((), ())),
            preferred_element_type=F32,
        )
    scores = jnp.where(matched[...] > 0.5, scores, 0.0)
    for k in range(top):
        rg_ref[k : k + 1, :] = jnp.sum(
            jnp.where(ids_ref[k : k + 1, :] == expert_of, scores, 0.0), axis=0, keepdims=True
        )
    finish.wait_recv()
    wg_ref[:, other_half] = fr[...]

    swap.wait_send()
    share.wait_send()
    give.wait_send()
    finish.wait_send()
    all_of(wf, wz_s, nz - 1)
    all_of(wf, wx_s, nz)
    for q in range(chunks):
        all_of(gin.at[q], g_s, rest)
        all_of(xs.at[q], rx_s, nz)
        all_of(zs.at[q], rz_s, nz - 1)
    all_of(arr, o_s, rest)


def solution(mesh):
    nz = mesh.shape["edp"] // 4
    ny = mesh.shape["ep"] // 2
    chunks = 2
    split = Mesh(mesh.devices.reshape(nz, 2, 2, ny, 2), AXES)

    def local(route_ids, route_weights, hidden, down_weight, cotangent):
        tokens, top = route_ids.shape
        ne, cap, ff = hidden.shape[2:]
        rows, features = down_weight.shape[1:]
        half = features // 2
        wide = half // chunks
        slots = ne * cap
        vmem = pl.BlockSpec(memory_space=pltpu.VMEM)
        away = pl.BlockSpec(memory_space=pltpu.HBM)
        dma = pltpu.SemaphoreType.DMA
        terms = (chunks, nz, 2 * rows, wide)
        outs = pl.pallas_call(
            functools.partial(kernel, (nz, ny, 2, min(5, nz // 2))),
            out_shape=(
                jax.ShapeDtypeStruct((tokens, features), BF16),
                jax.ShapeDtypeStruct((top, tokens), F32),
                jax.ShapeDtypeStruct((slots, ff), BF16),
                jax.ShapeDtypeStruct((rows, features), F32),
            ),
            in_specs=[vmem, vmem, away, away, away],
            out_specs=(vmem,) * 4,
            scratch_shapes=[
                pltpu.VMEM((tokens, features), BF16),
                pltpu.VMEM((rows, features), BF16),
                pltpu.VMEM((chunks, 2, ne, cap, wide), BF16),
                pltpu.VMEM((chunks, 2 * ne, cap, wide), BF16),
                pltpu.VMEM((2, ne, cap, half), BF16),
                pltpu.VMEM((2 * ne, cap, half), BF16),
                pltpu.VMEM((2, slots, ff), BF16),
                pltpu.VMEM((rows, half), BF16),
                pltpu.VMEM((2 * nz, 2 * rows, half), BF16),
                pltpu.VMEM((slots, ff), F32),
                pltpu.VMEM((slots, ff), F32),
                pltpu.VMEM((slots, ff), F32),
                pltpu.VMEM((chunks, nz, 2, 2 * rows, wide), F32),
                pltpu.VMEM(terms, BF16),
                pltpu.VMEM(terms, BF16),
                pltpu.VMEM(terms, BF16),
                pltpu.VMEM(terms, BF16),
                pltpu.VMEM((rows, half), F32),
                pltpu.VMEM((rows, half), F32),
                pltpu.VMEM((slots, tokens), F32),
                pltpu.VMEM((tokens, slots), F32),
                pltpu.SemaphoreType.REGULAR,
                dma, dma,
                dma, dma, dma,
                dma, dma,
                dma, dma((nz - 1,)), dma, dma,
                dma, dma((chunks,)), dma((chunks,)),
                dma, dma, dma,
                dma, dma,
                dma, dma((chunks, nz)),
                dma, dma((chunks,)),
                dma, dma,
            ],
            compiler_params=pltpu.CompilerParams(
                collective_id=0, has_side_effects=True, vmem_limit_bytes=40 * 2**20
            ),
        )(
            pltpu.with_memory_space_constraint(route_ids.T, pltpu.HBM),
            pltpu.with_memory_space_constraint(route_weights.T, pltpu.HBM),
            pltpu.with_memory_space_constraint(hidden.reshape(slots, ff), pltpu.HBM),
            pltpu.with_memory_space_constraint(down_weight.reshape(rows, features), pltpu.HBM),
            pltpu.with_memory_space_constraint(cotangent, pltpu.HBM),
        )
        out, route_grad, hidden_grad, weight_grad = outs
        return out, route_grad.T, hidden_grad.reshape(hidden.shape), weight_grad[None]

    placed = (P(AXES, None), P(AXES, None), P(EDP, EP, None, None, None), P(EP, EDP, None), P(AXES, None))
    return jax.shard_map(
        local,
        mesh=split,
        in_specs=placed,
        out_specs=(P(AXES, None), P(AXES, None), P(EDP, EP, None, None, None), P(EP, EDP, None)),
        check_vma=False,
    )
```

time: 85.1 us -> 78.7 us (0.925)
  local copies, waits for them, and re-layouts: 7.07 us -> 2.69 us
  Pallas kernels: 76.7 us -> 75.2 us
    unnamed x12 -> x4, local copies, waits for them, and re-layouts: 7.07 us -> 2.69 us
    pallas_call x1, Pallas kernels: 76.7 us -> 75.2 us  [local(): pl.pallas_call(functools.partial(kernel, (nz, ny, 2, min(5, nz // 2))), o...]
where the time goes in v2:
time: 78.7 us; the launch traced here: 78.5 us
  Pallas kernels  75.2 us (96%)
  local copies, waits for them, and re-layouts  2.69 us (3%)
    pallas_call x1, Pallas kernels, local(): pl.pallas_call(functools.partial(kernel, (nz, ny, 2, min(5, nz // 2))), o...  75.2 us
    unnamed x4, local copies, waits for them, and re-layouts  2.69 us

profile of v2, /device:TPU:1, one launch (start us, length us, event | category | flops | bytes accessed | tf_op | source)
XLA Modules:
  0.0 78.5 jit_solution(7141038471502302106)
XLA Ops:
  0.6 75.2 %shard_map.84 = (bf16[128,2048]{1,0:T(8,128)(2,1)S(1)}, f32[8,128]{1,0:T(8,128)S(1)}, bf16[256,384]{1,0:T(8,128)(2,1)S(1)}, f32[8,2048]{1,0:T(8,128)S(1)}) custom-call(s32[8,128]{1,0:T(8,128)} %bitcast.12, f32[8,128]{1,0:T(8,128)} %bitcast.13, bf16[256,384]{1,0:T(8,128)(2,1)} %bitcast.10, bf16[8,2048]{1,0:T(8,128)(2,1)} %bitcast.11, bf16[128,2048]{1,0:T(8,128)(2,1)} %cot_ref.1), custom_call_target="tpu_custom_call" | custom-call | tf_op jit(solution)/shard_map/pallas_call | solution.py:377
  75.8 0.8 %copy.13 = bf16[128,2048]{1,0:T(8,128)(2,1)} copy(bf16[128,2048]{1,0:T(8,128)(2,1)S(1)} %get-tuple-element.16) | data formatting | bytes 1048576
  76.6 0.6 copy.14
  77.2 0.7 copy.15
  77.9 0.6 copy.16

commit v3 on v2

--- a/solution.py
+++ b/solution.py
@@ -17,6 +17,11 @@
 
 
 ORDER = (1, -1, 4, -4, 2, -2, 3, -3, 5, -5, 6)
+
+
+FAR_FIRST = True
+OUT_FIRST = True
+CHUNKS = 1
 
 
 def centred(i, n):
@@ -80,7 +85,7 @@
     def tell_z(i, carry):
         zz = lax.rem(z + centred(i, nz), nz)
 
-        @pl.when((zz >= early) | jnp.logical_not(late))
+        @pl.when((zz >= early) | (zz > z))
         def _():
             tell(barrier, z=zz)
 
@@ -88,7 +93,7 @@
 
     lax.fori_loop(0, nz - 1, tell_z, 0)
     plane = (ny - 1) * nxh * 2 + (nxh - 1) * 2 + 2
-    peers = plane + jnp.where(late, nz - 1, early - 1)
+    peers = plane + jnp.where(late, nz - 1, z)
 
     load_cot = pltpu.make_async_copy(cot_ref, cot, cot_l)
     load_cot.start()
@@ -129,9 +134,10 @@
 
     pl.semaphore_wait(barrier, peers)
 
-    @pl.when(late)
-    def _():
-        for zz in range(early):
+    for zz in range(early):
+
+        @pl.when(z > zz)
+        def _():
             tell(clear, z=zz)
 
     load_w.wait()
@@ -168,17 +174,16 @@
 
     rest = 2 * ne - 1
     stay = [pltpu.make_async_copy(sg.at[q, c, me], gin.at[q, own_slot], g_l.at[q]) for q in range(chunks)]
-    near(sg.at[0], gin.at[0], g_s, g_r.at[0])
-    stay[0].start()
-    far(sg.at[0], gin.at[0], g_s, g_r.at[0])
-    share = remote(hid_ref, hidb.at[c], hid_s, hid_r, c=core)
-    share.start()
-    for q in range(1, chunks):
-        weigh(q)
+
+    def send_chunk(q):
+        if FAR_FIRST:
+            far(sg.at[q], gin.at[q], g_s, g_r.at[q])
         near(sg.at[q], gin.at[q], g_s, g_r.at[q])
         stay[q].start()
-        far(sg.at[q], gin.at[q], g_s, g_r.at[q])
-
+        if not FAR_FIRST:
+            far(sg.at[q], gin.at[q], g_s, g_r.at[q])
+
+    send_chunk(0)
     swap.wait_recv()
     mine = own_w[:, own_half].astype(F32)
     theirs = wsw[...].astype(F32)
@@ -186,19 +191,30 @@
     second = jnp.where(c == 0, theirs, mine)
     wf[chip] = jnp.concatenate([first, second], axis=0).astype(BF16)
     remote(wf.at[chip], wf.at[chip], wx_s, wx_r, xl=1 - xl).start()
-    mixing[...] = mix.T
-
-    @pl.when(jnp.logical_not(late))
-    def _():
-        pl.semaphore_wait(clear, nz - early)
 
     def pass_on(piece, d, step):
         remote(
             wf.at[piece], wf.at[piece], wz_s, wz_r.at[ORDER.index(d)], z=lax.rem(z + step + nz, nz)
         ).start()
 
-    for d in (4, -4, 1, -1):
-        pass_on(chip, d, d)
+    @pl.when(late)
+    def _():
+        for d in (4, -4, 1, -1):
+            pass_on(chip, d, d)
+
+    share = remote(hid_ref, hidb.at[c], hid_s, hid_r, c=core)
+    share.start()
+    for q in range(1, chunks):
+        weigh(q)
+        send_chunk(q)
+    mixing[...] = mix.T
+
+    @pl.when(jnp.logical_not(late))
+    def _():
+        pl.semaphore_wait(clear, nz - 1 - z)
+        for d in (4, -4, 1, -1):
+            pass_on(chip, d, d)
+
     last = chunks - 1
 
     for i, d in enumerate(ORDER):
@@ -267,19 +283,24 @@
 
     share.wait_recv()
     keep.wait()
+    stay_out = pltpu.make_async_copy(eo.at[c, me], arr.at[own_slot], o_l)
+    if OUT_FIRST:
+        all_of(wf, wx_r, nz)
+        outputs()
+        near(eo, arr, o_s, o_r)
+        stay_out.start()
     for q in range(chunks):
         all_of(gin.at[q], g_r.at[q], rest)
         stay[q].wait()
-        if q == last:
+        if q == last and not OUT_FIRST:
             near(eo, arr, o_s, o_r)
+            stay_out.start()
         products(q)
-        if q == 0:
+        if q == 0 and not OUT_FIRST:
             all_of(wf, wx_r, nz)
             outputs()
-        if q < chunks - 1:
+        if q < last:
             along_z(q)
-    stay_out = pltpu.make_async_copy(eo.at[c, me], arr.at[own_slot], o_l)
-    stay_out.start()
     far(eo, arr, o_s, o_r)
     along_z(last)
 
@@ -357,10 +378,15 @@
     all_of(arr, o_s, rest)
 
 
+def put(*refs):
+    for i in range(4):
+        refs[4 + i][...] = refs[i][...]
+
+
 def solution(mesh):
     nz = mesh.shape["edp"] // 4
     ny = mesh.shape["ep"] // 2
-    chunks = 2
+    chunks = CHUNKS
     split = Mesh(mesh.devices.reshape(nz, 2, 2, ny, 2), AXES)
 
     def local(route_ids, route_weights, hidden, down_weight, cotangent):
@@ -371,7 +397,7 @@
         wide = half // chunks
         slots = ne * cap
         vmem = pl.BlockSpec(memory_space=pltpu.VMEM)
-        away = pl.BlockSpec(memory_space=pltpu.HBM)
+        away = pl.BlockSpec(memory_space=pl.ANY)
         dma = pltpu.SemaphoreType.DMA
         terms = (chunks, nz, 2 * rows, wide)
         outs = pl.pallas_call(
@@ -428,7 +454,14 @@
             pltpu.with_memory_space_constraint(down_weight.reshape(rows, features), pltpu.HBM),
             pltpu.with_memory_space_constraint(cotangent, pltpu.HBM),
         )
-        out, route_grad, hidden_grad, weight_grad = outs
+        out, route_grad, hidden_grad, weight_grad = pl.pallas_call(
+            put,
+            out_shape=tuple(jax.ShapeDtypeStruct(o.shape, o.dtype) for o in outs),
+            in_specs=[vmem] * 4,
+            out_specs=(vmem,) * 4,
+            compiler_params=pltpu.CompilerParams(vmem_limit_bytes=8 * 2**20),
+            name="put",
+        )(*outs)
         return out, route_grad.T, hidden_grad.reshape(hidden.shape), weight_grad[None]
 
     placed = (P(AXES, None), P(AXES, None), P(EDP, EP, None, None, None), P(EP, EDP, None), P(AXES, None))

time: 78.7 us -> 68.9 us (0.88)
  Pallas kernels: 75.2 us -> 68 us
  local copies, waits for them, and re-layouts: 2.69 us -> 0 us
    pallas_call x1, Pallas kernels: 75.2 us -> 67.1 us  [local(): pl.pallas_call(functools.partial(kernel, (nz, ny, 2, min(5, nz // 2))), o...]
    unnamed x4 -> x0, local copies, waits for them, and re-layouts: 2.69 us -> none
    pallas_call x0 -> x1, Pallas kernels: none -> 0.93 us  [local(): pl.pallas_call(put, out_shape=tuple((jax.ShapeDtypeStruct(o.shape, o.dtyp...]
where the time goes in v3:
time: 68.9 us; the launch traced here: 68.7 us
  Pallas kernels  68 us (99%)
    pallas_call x1, Pallas kernels, local(): pl.pallas_call(functools.partial(kernel, (nz, ny, 2, min(5, nz // 2))), o...  67.1 us

profile of v3, /device:TPU:1, one launch (start us, length us, event | category | flops | bytes accessed | tf_op | source)
XLA Modules:
  0.0 68.7 jit_solution(6286082662610684974)
XLA Ops:
  0.6 67.1 %shard_map.84 = (bf16[128,2048]{1,0:T(8,128)(2,1)S(1)}, f32[8,128]{1,0:T(8,128)S(1)}, bf16[256,384]{1,0:T(8,128)(2,1)S(1)}, f32[8,2048]{1,0:T(8,128)S(1)}) custom-call(s32[8,128]{1,0:T(8,128)} %bitcast.9, f32[8,128]{1,0:T(8,128)} %bitcast.10, bf16[256,384]{1,0:T(8,128)(2,1)} %bitcast.7, bf16[8,2048]{1,0:T(8,128)(2,1)} %bitcast.8, bf16[128,2048]{1,0:T(8,128)(2,1)} %cot_ref.1), custom_call_target="tpu_custom_call" | custom-call | tf_op jit(solution)/shard_map/pallas_call | solution.py:403
  67.7 0.9 %put.1 = (bf16[128,2048]{1,0:T(8,128)(2,1)}, f32[8,128]{1,0:T(8,128)}, bf16[256,384]{1,0:T(8,128)(2,1)}, f32[8,2048]{1,0:T(8,128)}) custom-call(bf16[128,2048]{1,0:T(8,128)(2,1)S(1)} %get-tuple-element.12.refs_0_, f32[8,128]{1,0:T(8,128)S(1)} %get-tuple-element.13.refs_1_, bf16[256,384]{1,0:T(8,128)(2,1)S(1)} %get-tuple-element.14.refs_2_, ...), custom_call_target="tpu_custom_call" | custom-call | tf_op jit(solution)/shard_map/put/pallas_call | solution.py:457

commit v4 on v3

--- a/solution.py
+++ b/solution.py
@@ -16,10 +16,11 @@
 BF16 = jnp.bfloat16
 
 
-ORDER = (1, -1, 4, -4, 2, -2, 3, -3, 5, -5, 6)
-
-
-FAR_FIRST = True
+ORDER = (1, -1, 4, -4, 3, -3, 5, -5, 6, 2, -2)
+SIDE = (1, -1, 2, -2)
+CROSS = (4, -4, 3, -3, 5, -5, 6)
+
+
 OUT_FIRST = True
 CHUNKS = 1
 
@@ -34,9 +35,9 @@
     ids_ref, w_ref, hid_ref, wsh_ref, cot_ref,
     lo_ref, rg_ref, hg_ref, wg_ref,
     cot, own_w, sg, gin, eo, arr, hidb, wsw, wf, hgp, hgr, hgo, pf, xs, xr, zs, zr, fs, fr,
-    matched, mixing,
-    clear,
-    cot_l, ow_l, hid_s, hid_r, hid_l, wsw_s, wsw_r, wz_s, wz_r, wx_s, wx_r,
+    matched, mixing, sums,
+    clear, hello,
+    cot_l, ow_l, hid_s, hid_r, hid_l, wsw_s, wsw_r, wz_s, wz_r, wx_s, wx_r, wx_o, wy_r,
     g_s, g_r, g_l, o_s, o_r, o_l, hg_s, hg_r, rx_s, rx_r, rz_s, rz_r, f_s, f_r,
 ):
     nz, ny, nxh, early = sizes
@@ -65,35 +66,42 @@
         pltpu.make_async_copy(ref.at[pl.ds(0, count)], ref.at[pl.ds(0, count)], sem).wait()
 
     barrier = pltpu.get_barrier_semaphore()
-
-    def tell_y(i, carry):
-        yy = lax.rem(y + centred(i, ny), ny)
-        for x in range(nxh):
+    corner = (z == 0) & (xl == 0)
+    column = (xl == 0) & (c == 0) & (y == 0) & (xh == 0)
+    is_first = corner & column
+    group = corner & jnp.logical_not(is_first)
+    beside = (z == 0) & (xl == 1) & (c == 0) & (y == 0) & (xh == 0)
+    late = (z >= early) | is_first
+
+    @pl.when(jnp.logical_not(is_first))
+    def _():
+        def tell_y(i, carry):
+            yy = lax.rem(y + centred(i, ny), ny)
+            for x in range(nxh):
+                for h in range(2):
+                    tell(barrier, y=yy, xh=x, c=h)
+            return carry
+
+        lax.fori_loop(0, ny - 1, tell_y, 0)
+        for dx in range(1, nxh):
             for h in range(2):
-                tell(barrier, y=yy, xh=x, c=h)
-        return carry
-
-    lax.fori_loop(0, ny - 1, tell_y, 0)
-    for dx in range(1, nxh):
-        for h in range(2):
-            tell(barrier, xh=lax.rem(xh + dx, nxh), c=h)
-    tell(barrier, xl=1 - xl)
-    tell(barrier, c=core)
-
-    late = z >= early
+                tell(barrier, xh=lax.rem(xh + dx, nxh), c=h)
+        tell(barrier, xl=1 - xl)
+        tell(barrier, c=core)
 
     def tell_z(i, carry):
         zz = lax.rem(z + centred(i, nz), nz)
 
-        @pl.when((zz >= early) | (zz > z))
+        @pl.when((zz >= early) | ((zz > z) & jnp.logical_not(is_first)) | (column & (zz == 0)))
         def _():
             tell(barrier, z=zz)
 
         return carry
 
     lax.fori_loop(0, nz - 1, tell_z, 0)
-    plane = (ny - 1) * nxh * 2 + (nxh - 1) * 2 + 2
-    peers = plane + jnp.where(late, nz - 1, z)
+    plane = (ny - 1) * nxh * 2 + (nxh - 1) * 2 + 2 - jnp.where(group | beside, 1, 0)
+    ahead = z - jnp.where(column, 1, 0)
+    peers = plane + jnp.where(late, nz - 1, ahead)
 
     load_cot = pltpu.make_async_copy(cot_ref, cot, cot_l)
     load_cot.start()
@@ -119,7 +127,7 @@
     preceding = jnp.dot(names.astype(BF16), before, preferred_element_type=F32)
     match = jnp.where((names > 0.5) & (preceding == rank_of.astype(F32)), 1.0, 0.0)
     mix = match * chosen
-    matched[...] = match
+    matched[...] = match.reshape(ne, cap, tokens)
     selector = match.astype(BF16)
     slot_weight = jnp.sum(mix, axis=1, keepdims=True)
     load_cot.wait()
@@ -135,39 +143,67 @@
     pl.semaphore_wait(barrier, peers)
 
     for zz in range(early):
-
-        @pl.when(z > zz)
+        here = (z > zz) | (is_first & (zz > 0))
+        if zz == 0:
+            here = here & jnp.logical_not(column)
+
+        @pl.when(here)
         def _():
             tell(clear, z=zz)
+
+    @pl.when(is_first)
+    def _():
+        for yy in range(ny):
+            for x in range(nxh):
+                for h in range(2):
+                    if (yy, x, h) != (0, 0, 0):
+                        tell(hello, y=yy, xh=x, c=h)
+        tell(hello, xl=1 - xl)
 
     load_w.wait()
     other_half = pl.ds(pl.multiple_of(core * half, half), half)
     own_half = pl.ds(pl.multiple_of(c * half, half), half)
     swap = remote(own_w.at[:, other_half], wsw, wsw_s, wsw_r, c=core)
-    swap.start()
-
-    def near(src, dst, send, recv):
+
+    @pl.when(jnp.logical_not(group))
+    def _():
+        swap.start()
+
+    def near(src, dst, send, recv, skip=False):
+        def to(yy, h, where):
+            def go():
+                remote(src.at[h, yy * nxh + xh], dst.at[own_slot], send, recv, **where).start()
+
+            if skip:
+                pl.when(jnp.logical_not(corner & (yy == 0) & (xh == 0) & (h == 0)))(go)
+            else:
+                go()
+
         def ring(i, carry):
             yy = lax.rem(y + centred(i, ny), ny)
             for h in range(2):
-                remote(src.at[h, yy * nxh + xh], dst.at[own_slot], send, recv, y=yy, c=h).start()
+                to(yy, h, dict(y=yy, c=h))
             return carry
 
         lax.fori_loop(0, ny - 1, ring, 0)
-        remote(src.at[core, me], dst.at[own_slot], send, recv, c=core).start()
-
-    def far_step(i, src, dst, send, recv):
-        yy = lax.rem(y + centred(i, ny), ny)
-        for dx in range(1, nxh):
-            xx = lax.rem(xh + dx, nxh)
-            for h in range(2):
-                remote(
-                    src.at[h, yy * nxh + xx], dst.at[own_slot], send, recv, y=yy, xh=xx, c=h
-                ).start()
-
-    def far(src, dst, send, recv):
+        to(y, core, dict(c=core))
+
+    def far(src, dst, send, recv, skip=False):
         def ring(i, carry):
-            far_step(i, src, dst, send, recv)
+            yy = lax.rem(y + centred(i, ny), ny)
+            for dx in range(1, nxh):
+                xx = lax.rem(xh + dx, nxh)
+                for h in range(2):
+
+                    def go():
+                        remote(
+                            src.at[h, yy * nxh + xx], dst.at[own_slot], send, recv, y=yy, xh=xx, c=h
+                        ).start()
+
+                    if skip and h == 0:
+                        pl.when(jnp.logical_not(corner & (yy == 0) & (xx == 0)))(go)
+                    else:
+                        go()
             return carry
 
         lax.fori_loop(0, ny, ring, 0)
@@ -175,22 +211,32 @@
     rest = 2 * ne - 1
     stay = [pltpu.make_async_copy(sg.at[q, c, me], gin.at[q, own_slot], g_l.at[q]) for q in range(chunks)]
 
-    def send_chunk(q):
-        if FAR_FIRST:
-            far(sg.at[q], gin.at[q], g_s, g_r.at[q])
-        near(sg.at[q], gin.at[q], g_s, g_r.at[q])
+    def send_chunk(q, skip=False):
+        far(sg.at[q], gin.at[q], g_s, g_r.at[q], skip)
+        near(sg.at[q], gin.at[q], g_s, g_r.at[q], skip)
         stay[q].start()
-        if not FAR_FIRST:
-            far(sg.at[q], gin.at[q], g_s, g_r.at[q])
-
-    send_chunk(0)
+
+    send_chunk(0, True)
+
+    @pl.when(group | beside)
+    def _():
+        pl.semaphore_wait(hello, 1)
+
+    @pl.when(group)
+    def _():
+        remote(
+            sg.at[0, 0, 0], gin.at[0, own_slot], g_s, g_r.at[0],
+            z=z, xl=xl, c=c * 0, y=y * 0, xh=xh * 0,
+        ).start()
+        swap.start()
+
     swap.wait_recv()
     mine = own_w[:, own_half].astype(F32)
     theirs = wsw[...].astype(F32)
     first = jnp.where(c == 0, mine, theirs)
     second = jnp.where(c == 0, theirs, mine)
     wf[chip] = jnp.concatenate([first, second], axis=0).astype(BF16)
-    remote(wf.at[chip], wf.at[chip], wx_s, wx_r, xl=1 - xl).start()
+    remote(wf.at[chip], wf.at[chip], wx_s, wx_o, xl=1 - xl).start()
 
     def pass_on(piece, d, step):
         remote(
@@ -207,18 +253,30 @@
     for q in range(1, chunks):
         weigh(q)
         send_chunk(q)
-    mixing[...] = mix.T
+    mixing[...] = mix.reshape(ne, cap, tokens)
 
     @pl.when(jnp.logical_not(late))
     def _():
-        pl.semaphore_wait(clear, nz - 1 - z)
+        pl.semaphore_wait(clear, nz - 1 - ahead)
         for d in (4, -4, 1, -1):
             pass_on(chip, d, d)
 
     last = chunks - 1
 
+    def side(piece, d, step):
+        remote(
+            wf.at[piece], wf.at[piece], wz_s, wy_r.at[SIDE.index(d)], z=lax.rem(z + step + nz, nz)
+        ).start()
+
+    def piece_from(d, column):
+        return lax.rem(z - d + nz, nz) * 2 + column
+
+    remote(wf.at[chip], wf.at[chip], wx_s, wx_o, xl=1 - xl).wait_recv()
+    for d in (1, -1):
+        side(z * 2 + 1 - xl, d, d)
+
     for i, d in enumerate(ORDER):
-        at = lax.rem(z - d + nz, nz) * 2 + xl
+        at = piece_from(d, xl)
         remote(wf.at[at], wf.at[at], wz_s, wz_r.at[i], xl=1 - xl).wait_recv()
         if abs(d) == 1:
             pass_on(at, 2 * d, d)
@@ -231,7 +289,24 @@
             def _():
                 pass_on(at, 6, 2 * sign)
 
-        remote(wf.at[at], wf.at[at], wx_s, wx_r, xl=1 - xl).start()
+        if d in CROSS:
+            remote(wf.at[at], wf.at[at], wx_s, wx_r, xl=1 - xl).start()
+        if d == -4:
+            for k, e in enumerate(SIDE[:2]):
+                at = piece_from(e, 1 - xl)
+                remote(wf.at[at], wf.at[at], wz_s, wy_r.at[k], xl=1 - xl).wait_recv()
+                side(at, 2 * e, e)
+
+    for k, e in enumerate(SIDE[2:]):
+        at = piece_from(e, 1 - xl)
+        remote(wf.at[at], wf.at[at], wz_s, wy_r.at[2 + k], xl=1 - xl).wait_recv()
+
+    def taker(i):
+        others = nz - early
+        served = jnp.where(
+            i < early, lax.rem(z + i, early), early + lax.rem(z + 1 + i - 2 * early + others, others)
+        )
+        return jnp.where(z >= early, served, lax.rem(z + centred(i, nz), nz))
 
     def products(q):
         step = min(wide, 256)
@@ -250,7 +325,7 @@
         lax.fori_loop(0, wide // step, body, 0)
 
         def to_neighbour(i, carry):
-            to = lax.rem(z + centred(i, nz), nz)
+            to = taker(i)
             xs[q, to] = pf[q, to, 1 - xl].astype(BF16)
             remote(xs.at[q, to], xr.at[q, to], rx_s, rx_r.at[q, i], xl=1 - xl).start()
             return carry
@@ -259,7 +334,7 @@
 
     def along_z(q):
         def body(i, carry):
-            to = lax.rem(z + centred(i, nz), nz)
+            to = taker(i)
             remote(xs.at[q, to], xr.at[q, to], rx_s, rx_r.at[q, i], xl=1 - xl).wait_recv()
             zs[q, to] = (pf[q, to, xl] + xr[q, to].astype(F32)).astype(BF16)
             remote(zs.at[q, to], zr.at[q, z], rz_s, rz_r.at[q], z=to).start()
@@ -285,23 +360,23 @@
     keep.wait()
     stay_out = pltpu.make_async_copy(eo.at[c, me], arr.at[own_slot], o_l)
     if OUT_FIRST:
-        all_of(wf, wx_r, nz)
+        all_of(wf, wx_r, len(CROSS))
         outputs()
-        near(eo, arr, o_s, o_r)
+        near(eo, arr, o_s, o_r.at[0])
+        far(eo, arr, o_s, o_r.at[1])
         stay_out.start()
     for q in range(chunks):
         all_of(gin.at[q], g_r.at[q], rest)
         stay[q].wait()
         if q == last and not OUT_FIRST:
-            near(eo, arr, o_s, o_r)
+            near(eo, arr, o_s, o_r.at[0])
             stay_out.start()
         products(q)
         if q == 0 and not OUT_FIRST:
-            all_of(wf, wx_r, nz)
+            all_of(wf, wx_r, len(CROSS))
             outputs()
         if q < last:
             along_z(q)
-    far(eo, arr, o_s, o_r)
     along_z(last)
 
     def hidden_term(group):
@@ -320,6 +395,40 @@
     hgo[...] = hidden_term(c)
     give.wait_recv()
     hg_ref[...] = (hgo[...] + hgr[...]).astype(BF16)
+
+    def combine(column, first):
+        def rows_of(ref, base=0):
+            return jnp.concatenate([ref[base + e * nxh + column] for e in range(ny)], axis=0)
+
+        part_slots = ny * cap
+        mixed = rows_of(mixing).T
+        high = mixed.astype(BF16)
+        low = (mixed - high.astype(F32)).astype(BF16)
+        table = jnp.concatenate([high, low], axis=0)
+        scores = jnp.zeros((part_slots, tokens), F32)
+        for h in range(2):
+            part = rows_of(arr, h * ne)
+            cols = slice(h * half, (h + 1) * half)
+            both = jnp.dot(table, part, preferred_element_type=F32)
+            value = both[:tokens] + both[tokens:]
+            if first:
+                sums[:, cols] = value
+            else:
+                lo_ref[:, cols] = (sums[:, cols] + value).astype(BF16)
+            scores = scores + lax.dot_general(
+                part, cot[:, cols], (((1,), (1,)), ((), ())), preferred_element_type=F32
+            )
+        scores = jnp.where(rows_of(matched) > 0.5, scores, 0.0)
+        name = lax.broadcasted_iota(jnp.int32, (part_slots, tokens), 0) // cap * nxh + column
+        for k in range(top):
+            value = jnp.sum(
+                jnp.where(ids_ref[k : k + 1, :] == name, scores, 0.0), axis=0, keepdims=True
+            )
+            rg_ref[k : k + 1, :] = value if first else rg_ref[k : k + 1, :] + value
+
+    all_of(arr, o_r.at[0], 2 * ny - 1)
+    stay_out.wait()
+    combine(xh, True)
 
     rows = fs.shape[0]
     for q in range(chunks):
@@ -336,32 +445,8 @@
     finish = remote(fs, fr, f_s, f_r, c=core)
     finish.start()
 
-    all_of(arr, o_r, rest)
-    stay_out.wait()
-    mix = mixing[...]
-    high = mix.astype(BF16)
-    low = (mix - high.astype(F32)).astype(BF16)
-    table = jnp.concatenate([high, low], axis=0)
-    piece = min(half, 512)
-    for h in range(2):
-        for p in range(half // piece):
-            part = arr[h * ne : (h + 1) * ne, :, p * piece : (p + 1) * piece]
-            both = jnp.dot(table, part.reshape(slots, piece), preferred_element_type=F32)
-            at = h * half + p * piece
-            lo_ref[:, at : at + piece] = (both[:tokens] + both[tokens:]).astype(BF16)
-    scores = jnp.zeros((slots, tokens), F32)
-    for h in range(2):
-        scores = scores + lax.dot_general(
-            arr[h * ne : (h + 1) * ne].reshape(slots, half),
-            cot[:, h * half : (h + 1) * half],
-            (((1,), (1,)), ((), ())),
-            preferred_element_type=F32,
-        )
-    scores = jnp.where(matched[...] > 0.5, scores, 0.0)
-    for k in range(top):
-        rg_ref[k : k + 1, :] = jnp.sum(
-            jnp.where(ids_ref[k : k + 1, :] == expert_of, scores, 0.0), axis=0, keepdims=True
-        )
+    all_of(arr, o_r.at[1], 2 * ny)
+    combine(1 - xh, False)
     finish.wait_recv()
     wg_ref[:, other_half] = fr[...]
 
@@ -369,8 +454,8 @@
     share.wait_send()
     give.wait_send()
     finish.wait_send()
-    all_of(wf, wz_s, nz - 1)
-    all_of(wf, wx_s, nz)
+    all_of(wf, wz_s, nz - 1 + len(SIDE))
+    all_of(wf, wx_s, 1 + len(CROSS))
     for q in range(chunks):
         all_of(gin.at[q], g_s, rest)
         all_of(xs.at[q], rx_s, nz)
@@ -430,15 +515,17 @@
                 pltpu.VMEM(terms, BF16),
                 pltpu.VMEM((rows, half), F32),
                 pltpu.VMEM((rows, half), F32),
-                pltpu.VMEM((slots, tokens), F32),
-                pltpu.VMEM((tokens, slots), F32),
+                pltpu.VMEM((ne, cap, tokens), F32),
+                pltpu.VMEM((ne, cap, tokens), F32),
+                pltpu.VMEM((tokens, features), F32),
+                pltpu.SemaphoreType.REGULAR,
                 pltpu.SemaphoreType.REGULAR,
                 dma, dma,
                 dma, dma, dma,
                 dma, dma,
-                dma, dma((nz - 1,)), dma, dma,
+                dma, dma((nz - 1,)), dma, dma, dma, dma((4,)),
                 dma, dma((chunks,)), dma((chunks,)),
-                dma, dma, dma,
+                dma, dma((2,)), dma,
                 dma, dma,
                 dma, dma((chunks, nz)),
                 dma, dma((chunks,)),

time: 68.9 us -> 68.9 us (level)
  no operation moved by 1% of the time
where the time goes in v4:
time: 68.9 us; the launch traced here: 68.8 us
  Pallas kernels  68.1 us (99%)
    pallas_call x1, Pallas kernels, local(): pl.pallas_call(functools.partial(kernel, (nz, ny, 2, min(5, nz // 2))), o...  67.2 us

profile of v4, /device:TPU:1, one launch (start us, length us, event | category | flops | bytes accessed | tf_op | source)
XLA Modules:
  0.0 68.8 jit_solution(17706206127775015154)
XLA Ops:
  0.6 67.2 %shard_map.84 = (bf16[128,2048]{1,0:T(8,128)(2,1)S(1)}, f32[8,128]{1,0:T(8,128)S(1)}, bf16[256,384]{1,0:T(8,128)(2,1)S(1)}, f32[8,2048]{1,0:T(8,128)S(1)}) custom-call(s32[8,128]{1,0:T(8,128)} %bitcast.9, f32[8,128]{1,0:T(8,128)} %bitcast.10, bf16[256,384]{1,0:T(8,128)(2,1)} %bitcast.7, bf16[8,2048]{1,0:T(8,128)(2,1)} %bitcast.8, bf16[128,2048]{1,0:T(8,128)(2,1)} %cot_ref.1), custom_call_target="tpu_custom_call" | custom-call | tf_op jit(solution)/shard_map/pallas_call | solution.py:488
  67.8 0.9 %put.1 = (bf16[128,2048]{1,0:T(8,128)(2,1)}, f32[8,128]{1,0:T(8,128)}, bf16[256,384]{1,0:T(8,128)(2,1)}, f32[8,2048]{1,0:T(8,128)}) custom-call(bf16[128,2048]{1,0:T(8,128)(2,1)S(1)} %get-tuple-element.12.refs_0_, f32[8,128]{1,0:T(8,128)S(1)} %get-tuple-element.13.refs_1_, bf16[256,384]{1,0:T(8,128)(2,1)S(1)} %get-tuple-element.14.refs_2_, ...), custom_call_target="tpu_custom_call" | custom-call | tf_op jit(solution)/shard_map/put/pallas_call | solution.py:544
